TPU v7x, 768 devices: a whole 4x8x12 slice. The times are simulated.
768 devices in a mesh: gx: 96 (over x, z, core), yz: 8 (over y).
Axes of the slice: x: 4, y: 8, z: 12, core: 2. Of those that a mesh axis runs over, the one named last changes fastest.
Arguments:
- populations: float32 [19, 768, 64, 128], P(None, 'gx', 'yz'), may hold values from 0.01 to 0.2
- solid: int32 [768, 64, 128], P('gx', 'yz'), may hold values 0 or 1
- displacement: float32 [3, 835584], P(None, ('gx', 'yz')), may hold values from -3 to 3
- stiffness: float32 [835584], P(('gx', 'yz')), may hold values from 0.05 to 0.5
- marker_tile: int32 [835584, 1], P(('gx', 'yz')), may hold values from 0 to 15, as said below
- marker_site: int32 [835584], P(('gx', 'yz')), may hold values from 0 to 8191
Outputs:
- final_populations: float32 [19, 768, 64, 128], P(None, 'gx', 'yz')
- final_displacement: float32 [3, 835584], P(None, ('gx', 'yz'))
Inputs may be any that keep to these rules, and one draw needn't show every extreme that they name: `marker_tile`: among the rows of one device no value is named by more than 136 markers, and in every device's rows some value is named by exactly 136.
All inputs are finite; a program needn't handle non-finite values. No bound on the sum of `solid` on one device may be relied on, other than what follows from the above.
Results may differ from a plain program's by a relative error of at most 0.0003.
Values sent between devices are 32-bit elements; how exact they have to be, the bound alone decides.
A program may use at most 128 MiB of HBM per device.

v0:
```python
import functools

import jax
import jax.numpy as jnp
from jax import lax
from jax.experimental import pallas as pl
from jax.experimental.pallas import tpu as pltpu
from jax.sharding import PartitionSpec as P

MESH = pl.DeviceIdType.MESH
STEPS = 3
F32 = jnp.float32
BF16 = jnp.bfloat16
I32 = jnp.int32

lattice_dirs = [
    (0, 0, 0),
    (1, 0, 0),
    (-1, 0, 0),
    (0, 1, 0),
    (0, -1, 0),
    (0, 0, 1),
    (0, 0, -1),
    (1, 1, 0),
    (-1, -1, 0),
    (1, -1, 0),
    (-1, 1, 0),
    (1, 0, 1),
    (-1, 0, -1),
    (1, 0, -1),
    (-1, 0, 1),
    (0, 1, 1),
    (0, -1, -1),
    (0, 1, -1),
    (0, -1, 1),
]
lattice_weights = [1.0 / 3.0] + [1.0 / 18.0] * 6 + [1.0 / 36.0] * 12
relax_rate = 1.6
PUSH = 1.0 - 0.5 * relax_rate

X_FACE = [[1, 7, 9, 11, 13], [2, 8, 10, 12, 14]]
Y_FACE = [[3, 7, 10, 15, 17], [4, 8, 9, 16, 18]]
CORNER = [7, 8, 9, 10]

YZ = 8
TILES = 2 * YZ
LANES = 128
GROUPS = TILES + 1
SLOTS = GROUPS * LANES
BIN_PARTS = 3
STEP_PARTS = 2


def parts_of(value, count):
    parts = []
    rest = value
    for _ in range(count):
        part = rest.astype(BF16).astype(F32)
        parts.append(part)
        rest = rest - part
    return parts


def iota(shape, dim):
    return lax.broadcasted_iota(I32, shape, dim)


def spread(value):
    for shift in (8, 16, 32, 64):
        value = value + pltpu.roll(value, shift, 1)
    return value


def product(lhs, rhs, transposed):
    dims = (((1,), (1 if transposed else 0,)), ((), ()))
    return lax.dot_general(lhs, rhs, dims, preferred_element_type=F32)


def collide(popul, field, solid):
    density = popul[0]
    for index in range(1, 19):
        density = density + popul[index]
    moved = []
    for component in range(3):
        total = 0.5 * field[component]
        for index in range(1, 19, 2):
            offset = lattice_dirs[index][component]
            if offset > 0:
                total = total + (popul[index] - popul[index + 1])
            elif offset < 0:
                total = total - (popul[index] - popul[index + 1])
        moved.append(total)
    inverse = 1.0 / density
    speed = [total * inverse for total in moved]
    squared = speed[0] * speed[0] + speed[1] * speed[1] + speed[2] * speed[2]
    speed_field = speed[0] * field[0] + speed[1] * field[1] + speed[2] * field[2]
    dense = relax_rate * density
    base = dense - 1.5 * dense * squared - (3.0 * PUSH) * speed_field
    even = [(4.5 * relax_rate) * moved[c] + (9.0 * PUSH) * field[c] for c in range(3)]
    odd = [(3.0 * relax_rate) * moved[c] + (3.0 * PUSH) * field[c] for c in range(3)]
    wall = solid == 1
    keep = 1.0 - relax_rate
    result = [None] * 19
    result[0] = jnp.where(wall, popul[0], keep * popul[0] + lattice_weights[0] * base)

    def along(offsets, values):
        total = None
        for component in range(3):
            if offsets[component] != 0:
                term = values[component]
                if total is None:
                    total = term if offsets[component] > 0 else -term
                else:
                    total = total + term if offsets[component] > 0 else total - term
        return total

    for index in range(1, 19, 2):
        offsets = lattice_dirs[index]
        weight = lattice_weights[index]
        both = weight * (base + along(offsets, speed) * along(offsets, even))
        side = weight * along(offsets, odd)
        result[index] = jnp.where(wall, popul[index + 1], keep * popul[index] + (both + side))
        result[index + 1] = jnp.where(wall, popul[index], keep * popul[index + 1] + (both - side))
    return result, speed


def kernel(
    pop_hbm, solid_hbm, disp_ref, stiff_ref, tile_ref, site_ref,
    out_ref, dout_ref,
    start, solid, vals, tiles, hot, payload, recv, zhot, lhs, ubuf, field, slots,
    post, sx, sy, rx, ry, rc, back, ret,
    load_sem, put_send, put_recv, ret_send, ret_recv, halo_send, halo_recv,
):
    marks = disp_ref.shape[1]
    wide = vals.shape[1]
    blocks = wide // LANES
    n_gx = lax.axis_size("gx")
    g = lax.axis_index("gx")
    q = lax.axis_index("yz")

    def device(dg, dq):
        return (lax.rem(g + (dg + n_gx), n_gx), lax.rem(q + (dq + YZ), YZ))

    barrier = pltpu.get_barrier_semaphore()
    for dg in (-1, 0, 1):
        for dq in range(YZ):
            if (dg, dq) != (0, 0):
                pl.semaphore_signal(barrier, inc=1, device_id=device(dg, dq), device_id_type=MESH)

    load_pop = pltpu.make_async_copy(pop_hbm, start, load_sem.at[0])
    load_solid = pltpu.make_async_copy(solid_hbm, solid, load_sem.at[1])
    load_pop.start()
    load_solid.start()

    sub = iota((8, LANES), 0)
    lane_group = iota((8, LANES), 1) // 8
    own_group = lane_group == sub

    vals[...] = jnp.zeros_like(vals)
    tiles[...] = jnp.full_like(tiles, -1)
    tile = tile_ref[...]
    tiles[0:1, 0:marks] = (tile & YZ) + ((tile - q) & (YZ - 1))
    vals[0:1, 0:marks] = site_ref[...].astype(F32)
    vals[1:2, 0:marks] = stiff_ref[...]
    vals[2:5, 0:marks] = disp_ref[...]
    member = iota((TILES, wide), 0) == tiles[0:1, :]
    member_f = jnp.where(member, 1.0, 0.0)
    stacked = jnp.concatenate([member_f[:, b * LANES : (b + 1) * LANES] for b in range(blocks)], axis=0)
    upper = jnp.where(iota((LANES, LANES), 0) <= iota((LANES, LANES), 1), 1.0, 0.0).astype(BF16)
    counts = product(stacked.astype(BF16), upper, False)
    offset = jnp.full((TILES, 1), -1.0, F32)
    ranks = []
    for b in range(blocks):
        count = counts[b * TILES : (b + 1) * TILES, :]
        mine = member_f[:, b * LANES : (b + 1) * LANES]
        ranks.append(jnp.sum(mine * (count + offset), axis=0, keepdims=True))
        offset = offset + count[:, LANES - 1 : LANES]
    rank = jnp.concatenate(ranks, axis=1).astype(I32)
    row = iota((2 * LANES, wide), 0)
    wanted = jnp.where(row < LANES, row, LANES + (row & 7))
    hot[...] = jnp.where(wanted == rank, 1.0, 0.0).astype(BF16)

    binned = None
    for part in parts_of(vals[...], BIN_PARTS):
        left = jnp.concatenate(
            [jnp.where(member[k : k + 1, :], part, 0.0) for k in range(TILES)], axis=0
        ).astype(BF16)
        term = product(left, hot[...], True)
        binned = term if binned is None else binned + term
    for k in range(TILES):
        main = binned[k * 8 : (k + 1) * 8, 0:LANES]
        more = binned[k * 8 : (k + 1) * 8, LANES : 2 * LANES]
        more = jnp.sum(jnp.where(own_group, more, 0.0), axis=0, keepdims=True)
        payload[k] = jnp.where(sub == 5, more, main)

    pl.semaphore_wait(barrier, 3 * YZ - 1)

    puts = []
    for k in reversed(range(1, TILES)):
        put = pltpu.make_async_remote_copy(
            src_ref=payload.at[k],
            dst_ref=recv.at[k],
            send_sem=put_send.at[k],
            recv_sem=put_recv.at[k],
            device_id=device(k // YZ, k % YZ),
            device_id_type=MESH,
        )
        put.start()
        puts.append(put)
    load_pop.wait()
    load_solid.wait()
    for put in puts:
        put.wait_recv()

    tail = jnp.zeros((8, LANES), F32)
    for k in range(TILES):
        block = payload[0] if k == 0 else recv[k]
        slots[k] = block
        more = jnp.where(own_group, jnp.broadcast_to(block[5:6, :], (8, LANES)), 0.0)
        tail = tail + jnp.where(lane_group == k, spread(more), 0.0)
    slots[TILES] = tail
    rows32 = iota((32, LANES), 0)
    for k in range(GROUPS):
        site = slots[k][0:1, :].astype(I32)
        place = ((site >> 12) << 7) + (site & 127)
        zhot[:, k * LANES : (k + 1) * LANES] = jnp.where(
            iota((2 * LANES, LANES), 0) == place, 1.0, 0.0
        ).astype(BF16)

    def row_mask(block):
        return rows32 == ((block[0:1, :].astype(I32) >> 7) & 31)

    def deposit():
        for k in range(GROUPS):
            block = slots[k]
            mask = row_mask(block)
            force = -block[1:2, :] * block
            for number, part in enumerate(parts_of(force, STEP_PARTS)):
                for c in range(3):
                    top = number * 96 + c * 32
                    lhs[top : top + 32, k * LANES : (k + 1) * LANES] = jnp.where(
                        mask, part[2 + c : 3 + c, :], 0.0
                    ).astype(BF16)
        result = product(lhs[...], zhot[...], True)
        total = result[0:96, :]
        for number in range(1, STEP_PARTS):
            total = total + result[number * 96 : (number + 1) * 96, :]
        field[...] = total

    def gather():
        left = jnp.concatenate([part.astype(BF16) for part in parts_of(ubuf[...], STEP_PARTS)], axis=0)
        for k in range(GROUPS):
            block = slots[k]
            mask = row_mask(block)
            picked = product(left, zhot[:, k * LANES : (k + 1) * LANES], False)
            total = picked[0:96, :]
            for number in range(1, STEP_PARTS):
                total = total + picked[number * 96 : (number + 1) * 96, :]
            for c in range(3):
                speed = jnp.sum(
                    jnp.where(mask, total[c * 32 : (c + 1) * 32, :], 0.0), axis=0, keepdims=True
                )
                block = block + jnp.where(sub == 2 + c, speed, 0.0)
            slots[k] = block

    def pulled(step, index, a):
        cx, cy, cz = lattice_dirs[index]
        x_side = 0 if cx > 0 else 1
        y_side = 0 if cy > 0 else 1
        source = a - cx
        inside = 0 <= source < 8
        if inside:
            value = post[step % 2, index, source]
        else:
            value = rx[step, x_side, X_FACE[x_side].index(index)]
        if cy != 0:
            if inside:
                other = jnp.broadcast_to(
                    ry[step, y_side, Y_FACE[y_side].index(index), source : source + 1, :], (8, LANES)
                )
            else:
                other = rc[step, CORNER.index(index)]
            value = jnp.where(sub == (7 if cy > 0 else 0), other, value)
            value = pltpu.roll(value, cy % 8, 0)
        if cz != 0:
            value = pltpu.roll(value, cz % LANES, 1)
        return value

    def halo(step, which, src, dst, dg, dq):
        return pltpu.make_async_remote_copy(
            src_ref=src,
            dst_ref=dst,
            send_sem=halo_send.at[step * 8 + which],
            recv_sem=halo_recv.at[step * 8 + which],
            device_id=device(dg, dq),
            device_id_type=MESH,
        )

    def slice_step(step, a):
        if step == 0:
            popul = [start[index, a] for index in range(19)]
        else:
            popul = [pulled(step - 1, index, a) for index in range(19)]
        low = (a % 4) * 8
        high = (a // 4) * LANES
        fields = [field[c * 32 + low : c * 32 + low + 8, high : high + LANES] for c in range(3)]
        result, speed = collide(popul, fields, solid[a])
        for c in range(3):
            ubuf[c * 32 + low : c * 32 + low + 8, high : high + LANES] = speed[c]
        for index in range(19):
            post[step % 2, index, a] = result[index]
        for side, edge in ((0, 7), (1, 0)):
            if a == edge:
                for place, index in enumerate(X_FACE[side]):
                    sx[step, side, place] = result[index]
            for place, index in enumerate(Y_FACE[side]):
                sy[step, side, place, a : a + 1, :] = result[index][edge : edge + 1, :]

    returns = []
    sent = []
    deposit()
    for step in range(STEPS):
        copies = []
        slice_step(step, 0)
        slice_step(step, 7)
        for number, index in enumerate(CORNER):
            cx, cy, _ = lattice_dirs[index]
            side = 0 if cx > 0 else 1
            copies.append(
                halo(step, number, sx.at[step, side, X_FACE[side].index(index)], rc.at[step, number], cx, cy)
            )
            copies[-1].start()
        for side, dg in ((0, 1), (1, -1)):
            copies.append(halo(step, 4 + side, sx.at[step, side], rx.at[step, side], dg, 0))
            copies[-1].start()
        for a in range(1, 7):
            slice_step(step, a)
        for side, dq in ((0, 1), (1, -1)):
            copies.append(halo(step, 6 + side, sy.at[step, side], ry.at[step, side], 0, dq))
            copies[-1].start()
        gather()
        if step < STEPS - 1:
            deposit()
        else:
            tail = slots[TILES]
            for k in reversed(range(TILES)):
                more = spread(jnp.where(lane_group == k, tail, 0.0))
                more = jnp.sum(jnp.where(own_group, more, 0.0), axis=0, keepdims=True)
                block = jnp.where(sub == 5, more, slots[k])
                if k == 0:
                    ret[0] = block
                else:
                    back[k] = block
                    copy = pltpu.make_async_remote_copy(
                        src_ref=back.at[k],
                        dst_ref=ret.at[k],
                        send_sem=ret_send.at[k],
                        recv_sem=ret_recv.at[k],
                        device_id=device(-(k // YZ), -(k % YZ)),
                        device_id_type=MESH,
                    )
                    copy.start()
                    returns.append(copy)
        for copy in copies:
            copy.wait_recv()
        sent.extend(copies)

    for a in range(8):
        for index in range(19):
            out_ref[index, a] = pulled(STEPS - 1, index, a)

    for copy in returns:
        copy.wait_recv()
    lefts = []
    for k in range(TILES):
        block = ret[k]
        more = jnp.where(own_group, jnp.broadcast_to(block[5:6, :], (8, LANES)), 0.0)
        lefts.append(jnp.concatenate([block, more], axis=1))
    left = jnp.concatenate(lefts, axis=0)
    taken = None
    for part in parts_of(left, BIN_PARTS):
        term = product(part.astype(BF16), hot[...], False)
        taken = term if taken is None else taken + term
    member = iota((TILES, wide), 0) == tiles[0:1, :]
    final = None
    for k in range(TILES):
        term = jnp.where(member[k : k + 1, :], taken[k * 8 : (k + 1) * 8, :], 0.0)
        final = term if final is None else final + term
    dout_ref[...] = final[2:5, 0:marks]
    for copy in puts + sent + returns:
        copy.wait_send()


def body(populations, solid, displacement, stiffness, marker_tile, marker_site):
    marks = displacement.shape[1]
    wide = -(-marks // LANES) * LANES
    vmem = pl.BlockSpec(memory_space=pltpu.VMEM)
    hbm = pl.BlockSpec(memory_space=pl.ANY)
    dma = pltpu.SemaphoreType.DMA
    return pl.pallas_call(
        kernel,
        out_shape=(
            jax.ShapeDtypeStruct(populations.shape, F32),
            jax.ShapeDtypeStruct(displacement.shape, F32),
        ),
        in_specs=[hbm, hbm, vmem, vmem, vmem, vmem],
        out_specs=(vmem, vmem),
        scratch_shapes=[
            pltpu.VMEM(populations.shape, F32),
            pltpu.VMEM(solid.shape, I32),
            pltpu.VMEM((8, wide), F32),
            pltpu.VMEM((8, wide), I32),
            pltpu.VMEM((2 * LANES, wide), BF16),
            pltpu.VMEM((TILES, 8, LANES), F32),
            pltpu.VMEM((TILES, 8, LANES), F32),
            pltpu.VMEM((2 * LANES, SLOTS), BF16),
            pltpu.VMEM((96 * STEP_PARTS, SLOTS), BF16),
            pltpu.VMEM((96, 2 * LANES), F32),
            pltpu.VMEM((96, 2 * LANES), F32),
            pltpu.VMEM((GROUPS, 8, LANES), F32),
            pltpu.VMEM((2,) + populations.shape, F32),
            pltpu.VMEM((STEPS, 2, 5, 8, LANES), F32),
            pltpu.VMEM((STEPS, 2, 5, 8, LANES), F32),
            pltpu.VMEM((STEPS, 2, 5, 8, LANES), F32),
            pltpu.VMEM((STEPS, 2, 5, 8, LANES), F32),
            pltpu.VMEM((STEPS, 4, 8, LANES), F32),
            pltpu.VMEM((TILES, 8, LANES), F32),
            pltpu.VMEM((TILES, 8, LANES), F32),
            dma((2,)),
            dma((TILES,)),
            dma((TILES,)),
            dma((TILES,)),
            dma((TILES,)),
            dma((STEPS * 8,)),
            dma((STEPS * 8,)),
        ],
        compiler_params=pltpu.CompilerParams(collective_id=0, has_side_effects=True),
        name="lattice_steps",
    )(
        populations,
        solid,
        displacement,
        stiffness.reshape(1, -1),
        marker_tile.reshape(1, -1),
        marker_site.reshape(1, -1),
    )


def solution(mesh):
    in_specs = (
        P(None, "gx", "yz", None),
        P("gx", "yz", None),
        P(None, ("gx", "yz")),
        P(("gx", "yz")),
        P(("gx", "yz"), None),
        P(("gx", "yz")),
    )
    out_specs = (P(None, "gx", "yz", None), P(None, ("gx", "yz")))
    return jax.shard_map(body, mesh=mesh, in_specs=in_specs, out_specs=out_specs, check_vma=False)
```

profile of v0, /device:TPU:8, one launch (start us, length us, event | category | flops | bytes accessed | tf_op | source)
XLA Modules:
  0.0 49.4 jit_solution(7172503371485100)
XLA Ops:
  0.6 0.0 copy-start.1
  0.6 1.3 %reshape.13.stiff_ref = f32[1,1088]{1,0:T(1,128)} reshape(f32[1088]{0:T(1024)} %param.9) | data formatting | bytes 8704 | tf_op jit(solution)/shard_map/reshape | solution.py:443
  1.9 0.0 copy-done.1
  1.9 0.6 %reshape.15.site_ref = s32[1,1088]{1,0:T(1,128)} reshape(s32[1088]{0:T(1024)S(1)} %copy-done.1) | data formatting | bytes 8704 | tf_op jit(solution)/shard_map/reshape | solution.py:445
  2.5 44.3 %lattice_steps.1 = (f32[19,8,8,128]{3,2,1,0:T(8,128)}, f32[3,1088]{1,0:T(4,128)}) custom-call(f32[19,8,8,128]{3,2,1,0:T(8,128)} %pop_hbm.1, s32[8,8,128]{2,1,0:T(8,128)} %solid_hbm.1, f32[3,1088]{1,0:T(4,128)} %disp_ref.1, f32[1,1088]{1,0:T(1,128)} %reshape.13.stiff_ref, s32[1,1088]{1,0:T(1,128)} %bitcast.1, s32[1,1088]{1,0:T(1,128)} %reshape.15.site_ref), custom_call_target="tpu_custom_call" | custom-call | tf_op jit(solution)/shard_map/lattice_steps/pallas_call | solution.py:400
  46.9 0.0 copy-start
  46.9 2.0 %copy.10 = f32[19,8,8,128]{3,2,1,0:T(8,128)} copy(f32[19,8,8,128]{3,2,1,0:T(8,128)} %get-tuple-element.4) | data formatting | bytes 1245184
  48.8 0.0 copy-done
  48.8 0.6 %copy.11 = f32[3,1088]{1,0:T(4,128)} copy(f32[3,1088]{1,0:T(4,128)S(1)} %copy-done) | data formatting | bytes 26112
Async XLA Ops:
  0.6 1.3 %copy-start.1 = (s32[1088]{0:T(1024)S(1)}, s32[1088]{0:T(1024)}, u32[]{:S(2)}) copy-start(s32[1088]{0:T(1024)} %param.11) | copy-start | bytes 13060
  46.9 2.0 %copy-start = (f32[3,1088]{1,0:T(4,128)S(1)}, f32[3,1088]{1,0:T(4,128)}, u32[]{:S(2)}) copy-start(f32[3,1088]{1,0:T(4,128)} %get-tuple-element.5) | copy-start | bytes 39172
where the time goes:
time: 49.7 us; the launch traced here: 49.4 us
  Pallas kernels  44.3 us (89%)
  local copies, waits for them, and re-layouts  4.47 us (9%)
  between operations  0.66 us (1%)
    pallas_call x1, Pallas kernels, body(): pl.pallas_call(kernel, out_shape=(jax.ShapeDtypeStruct(populations.shape,...  44.3 us
    unnamed x6, local copies, waits for them, and re-layouts  2.58 us
    reshape x1, local copies, waits for them, and re-layouts, body(): stiffness.reshape(1, -1)  1.3 us

commit v1 on v0

v1 whole, which is shorter than its diff:
```python
import functools

import jax
import jax.numpy as jnp
from jax import lax
from jax.experimental import pallas as pl
from jax.experimental.pallas import tpu as pltpu
from jax.sharding import PartitionSpec as P

MESH = pl.DeviceIdType.MESH
STEPS = 3
F32 = jnp.float32
BF16 = jnp.bfloat16
I32 = jnp.int32

lattice_dirs = [
    (0, 0, 0),
    (1, 0, 0),
    (-1, 0, 0),
    (0, 1, 0),
    (0, -1, 0),
    (0, 0, 1),
    (0, 0, -1),
    (1, 1, 0),
    (-1, -1, 0),
    (1, -1, 0),
    (-1, 1, 0),
    (1, 0, 1),
    (-1, 0, -1),
    (1, 0, -1),
    (-1, 0, 1),
    (0, 1, 1),
    (0, -1, -1),
    (0, 1, -1),
    (0, -1, 1),
]
lattice_weights = [1.0 / 3.0] + [1.0 / 18.0] * 6 + [1.0 / 36.0] * 12
relax_rate = 1.6
PUSH = 1.0 - 0.5 * relax_rate

X_FACE = [[1, 7, 9, 11, 13], [2, 8, 10, 12, 14]]
Y_FACE = [[3, 7, 10, 15, 17], [4, 8, 9, 16, 18]]
CORNER = [7, 8, 9, 10]

YZ = 8
TILES = 2 * YZ
LANES = 128
GROUPS = TILES + 1
SLOTS = GROUPS * LANES
BIN_PARTS = 2
PUT_ROWS = 6
STEP_PARTS = 2


def parts_of(value, count):
    parts = []
    rest = value
    for _ in range(count):
        part = rest.astype(BF16).astype(F32)
        parts.append(part)
        rest = rest - part
    return parts


def iota(shape, dim):
    return lax.broadcasted_iota(I32, shape, dim)


def spread(value):
    for shift in (8, 16, 32, 64):
        value = value + pltpu.roll(value, shift, 1)
    return value


def product(lhs, rhs, transposed):
    dims = (((1,), (1 if transposed else 0,)), ((), ()))
    return lax.dot_general(lhs, rhs, dims, preferred_element_type=F32)


def collide(popul, field, solid):
    density = popul[0]
    for index in range(1, 19):
        density = density + popul[index]
    moved = []
    for component in range(3):
        total = 0.5 * field[component]
        for index in range(1, 19, 2):
            offset = lattice_dirs[index][component]
            if offset > 0:
                total = total + (popul[index] - popul[index + 1])
            elif offset < 0:
                total = total - (popul[index] - popul[index + 1])
        moved.append(total)
    inverse = 1.0 / density
    speed = [total * inverse for total in moved]
    squared = speed[0] * speed[0] + speed[1] * speed[1] + speed[2] * speed[2]
    speed_field = speed[0] * field[0] + speed[1] * field[1] + speed[2] * field[2]
    dense = relax_rate * density
    base = dense - 1.5 * dense * squared - (3.0 * PUSH) * speed_field
    even = [(4.5 * relax_rate) * moved[c] + (9.0 * PUSH) * field[c] for c in range(3)]
    odd = [(3.0 * relax_rate) * moved[c] + (3.0 * PUSH) * field[c] for c in range(3)]
    wall = solid == 1
    keep = 1.0 - relax_rate
    result = [None] * 19
    result[0] = jnp.where(wall, popul[0], keep * popul[0] + lattice_weights[0] * base)

    def along(offsets, values):
        total = None
        for component in range(3):
            if offsets[component] != 0:
                term = values[component]
                if total is None:
                    total = term if offsets[component] > 0 else -term
                else:
                    total = total + term if offsets[component] > 0 else total - term
        return total

    for index in range(1, 19, 2):
        offsets = lattice_dirs[index]
        weight = lattice_weights[index]
        both = weight * (base + along(offsets, speed) * along(offsets, even))
        side = weight * along(offsets, odd)
        result[index] = jnp.where(wall, popul[index + 1], keep * popul[index] + (both + side))
        result[index + 1] = jnp.where(wall, popul[index], keep * popul[index + 1] + (both - side))
    return result, speed


def kernel(
    pop_hbm, solid_hbm, disp_hbm, stiff_hbm, tile_hbm, site_hbm,
    out_ref, dout_ref,
    start, solid, disp, stiff, tile_in, site_in, vals, hot, payload, recv, zhot, lhs, usum, field, slots,
    post, edges, halos, back, ret,
    load_sem, put_send, put_recv, ret_send, ret_recv, halo_send, halo_recv,
):
    marks = disp_hbm.shape[1]
    wide = vals.shape[1]
    blocks = wide // LANES
    n_gx = lax.axis_size("gx")
    g = lax.axis_index("gx")
    q = lax.axis_index("yz")
    g_of = {0: g, 1: lax.rem(g + 1, n_gx), -1: lax.rem(g + (n_gx - 1), n_gx)}
    q_of = [q if dq == 0 else (q + dq) & (YZ - 1) for dq in range(YZ)]

    def device(dg, dq):
        return (g_of[dg], q_of[dq % YZ])

    far_first = (4, 3, 5, 2, 6, 1, 7, 0)
    barrier = pltpu.get_barrier_semaphore()
    for dq in far_first:
        for dg in (1, -1, 0):
            if (dg, dq) != (0, 0):
                pl.semaphore_signal(barrier, inc=1, device_id=device(dg, dq), device_id_type=MESH)

    loads = [
        pltpu.make_async_copy(src, dst, load_sem.at[number])
        for number, (src, dst) in enumerate(
            (
                (tile_hbm, tile_in),
                (site_hbm, site_in),
                (stiff_hbm, stiff),
                (disp_hbm, disp),
                (solid_hbm, solid),
                (pop_hbm, start),
            )
        )
    ]
    for load in loads:
        load.start()

    sub = iota((8, LANES), 0)
    lane_group = iota((8, LANES), 1) // 8
    own_group = lane_group == sub

    vals[...] = jnp.zeros_like(vals)
    vals[6:7, :] = jnp.full((1, wide), -1.0, F32)
    upper = jnp.where(iota((LANES, LANES), 0) <= iota((LANES, LANES), 1), 1.0, 0.0).astype(BF16)
    for load in loads[0:4]:
        load.wait()
    tile = tile_in[...]
    vals[6:7, 0:marks] = ((tile & YZ) + ((tile - q) & (YZ - 1))).astype(F32)
    vals[0:1, 0:marks] = site_in[...].reshape(1, marks).astype(F32)
    stiffness = stiff[...].reshape(1, marks)
    vals[1:2, 0:marks] = stiffness
    vals[2:5, 0:marks] = -stiffness * disp[...]
    tile8 = jnp.broadcast_to(vals[6:7, :].astype(I32), (8, wide))
    sub_wide = iota((8, wide), 0)
    member = [jnp.where(tile8 == sub_wide + 8 * half, 1.0, 0.0) for half in range(2)]
    member = jnp.concatenate(member, axis=0)
    stacked = jnp.concatenate([member[:, b * LANES : (b + 1) * LANES] for b in range(blocks)], axis=0)
    counts = product(stacked.astype(BF16), upper, False)
    offset = jnp.full((TILES, 1), -1.0, F32)
    ranks = []
    for b in range(blocks):
        count = counts[b * TILES : (b + 1) * TILES, :]
        mine = member[:, b * LANES : (b + 1) * LANES]
        ranks.append(jnp.sum(mine * (count + offset), axis=0, keepdims=True))
        offset = offset + count[:, LANES - 1 : LANES]
    rank8 = jnp.broadcast_to(jnp.concatenate(ranks, axis=1).astype(I32), (8, wide))
    for top in range(0, LANES, 16):
        pair = [jnp.where(sub_wide + (top + more) == rank8, 1.0, 0.0) for more in (0, 8)]
        hot[top : top + 16, :] = jnp.concatenate(pair, axis=0).astype(BF16)
    over = jnp.where(sub_wide + LANES == rank8, 1.0, 0.0)
    over = jnp.concatenate([over, over], axis=0).astype(BF16)
    for top in range(LANES, 2 * LANES, 16):
        hot[top : top + 16, :] = over

    value = jnp.where(sub_wide < 5, vals[...], 0.0)
    binned = None
    for part in parts_of(value, BIN_PARTS):
        left = jnp.concatenate([jnp.where(tile8 == k, part, 0.0) for k in range(TILES)], axis=0)
        term = product(left.astype(BF16), hot[...], True)
        binned = term if binned is None else binned + term
    for k in range(TILES):
        main = binned[k * 8 : (k + 1) * 8, 0:LANES]
        more = binned[k * 8 : (k + 1) * 8, LANES : 2 * LANES]
        more = jnp.sum(jnp.where(own_group, more, 0.0), axis=0, keepdims=True)
        payload[k] = jnp.where(sub == 5, more, main)

    pl.semaphore_wait(barrier, 3 * YZ - 1)

    def whole(buffer, sem):
        pltpu.make_async_copy(buffer, buffer, sem).wait()

    for half in (1, 0):
        for dq in far_first:
            k = half * YZ + dq
            if k != 0:
                pltpu.make_async_remote_copy(
                    src_ref=payload.at[k, pl.ds(0, PUT_ROWS)],
                    dst_ref=recv.at[k, pl.ds(0, PUT_ROWS)],
                    send_sem=put_send,
                    recv_sem=put_recv.at[half],
                    device_id=device(half, dq),
                    device_id_type=MESH,
                ).start()

    rows32 = iota((32, LANES), 0)

    def place_group(k, block):
        site = block[0:1, :].astype(I32)
        place = ((site >> 12) << 7) + (site & 127)
        zhot[:, k * LANES : (k + 1) * LANES] = jnp.where(
            iota((2 * LANES, LANES), 0) == place, 1.0, 0.0
        ).astype(BF16)
        mask = rows32 == ((site >> 7) & 31)
        for number, part in enumerate(parts_of(block, STEP_PARTS)):
            for c in range(4):
                top = (number * 4 + c) * 32
                lhs[top : top + 32, k * LANES : (k + 1) * LANES] = jnp.where(
                    mask, part[1 + c : 2 + c, :], 0.0
                ).astype(BF16)

    tail = jnp.zeros((8, LANES), F32)
    for half in range(2):
        first = 1 if half == 0 else YZ
        whole(recv.at[pl.ds(first, (half + 1) * YZ - first), pl.ds(0, PUT_ROWS)], put_recv.at[half])
        for k in range(half * YZ, (half + 1) * YZ):
            block = payload[0] if k == 0 else recv[k]
            slots[k] = block
            more = jnp.where(own_group, jnp.broadcast_to(block[5:6, :], (8, LANES)), 0.0)
            tail = tail + jnp.where(lane_group == k, spread(more), 0.0)
            place_group(k, block)
    slots[TILES] = tail
    place_group(TILES, tail)
    result = product(lhs[...], zhot[...], True)
    total = result[0:128, :]
    for number in range(1, STEP_PARTS):
        total = total + result[number * 128 : (number + 1) * 128, :]
    field[...] = total
    for load in loads[4:]:
        load.wait()

    def pulled(step, index, a):
        cx, cy, cz = lattice_dirs[index]
        x_side = 0 if cx > 0 else 1
        y_side = 0 if cy > 0 else 1
        source = a - cx
        inside = 0 <= source < 8
        if inside:
            value = post[step % 2, index, source]
        else:
            value = halos[step, 5 * x_side + X_FACE[x_side].index(index)]
        if cy != 0:
            if inside:
                tile_of = 10 + 4 + 5 * y_side + Y_FACE[y_side].index(index)
                other = jnp.broadcast_to(halos[step, tile_of, source : source + 1, :], (8, LANES))
            else:
                other = halos[step, 10 + CORNER.index(index)]
            value = jnp.where(sub == (7 if cy > 0 else 0), other, value)
            value = pltpu.roll(value, cy % 8, 0)
        if cz != 0:
            value = pltpu.roll(value, cz % LANES, 1)
        return value

    def halo(step, src, first, count, dg, dq):
        pltpu.make_async_remote_copy(
            src_ref=edges.at[step, pl.ds(src, count)],
            dst_ref=halos.at[step, pl.ds(first, count)],
            send_sem=halo_send.at[step],
            recv_sem=halo_recv.at[step, 0 if first < 14 else 1],
            device_id=device(dg, dq),
            device_id_type=MESH,
        ).start()

    def send_x(step):
        for number, index in enumerate(CORNER):
            cx, cy, _ = lattice_dirs[index]
            side = 0 if cx > 0 else 1
            halo(step, 5 * side + X_FACE[side].index(index), 10 + number, 1, cx, cy)
        for side, dg in ((0, 1), (1, -1)):
            halo(step, 5 * side, 5 * side, 5, dg, 0)

    def send_y(step):
        for side, dq in ((0, 1), (1, -1)):
            halo(step, 10 + 5 * side, 14 + 5 * side, 5, 0, dq)

    def slice_step(step, a):
        if step == 0:
            popul = [start[index, a] for index in range(19)]
        else:
            popul = [pulled(step - 1, index, a) for index in range(19)]
        low = (a % 4) * 8
        high = (a // 4) * LANES
        stiff_sum, *forces = [field[c * 32 + low : c * 32 + low + 8, high : high + LANES] for c in range(4)]
        result, speed = collide(popul, forces, solid[a])
        for c in range(3):
            place = (slice(c * 32 + low, c * 32 + low + 8), slice(high, high + LANES))
            usum[place] = speed[c] if step == 0 else usum[place] + speed[c]
            if step < STEPS - 1:
                field[32 + c * 32 + low : 32 + c * 32 + low + 8, high : high + LANES] = (
                    forces[c] - stiff_sum * speed[c]
                )
        for index in range(19):
            post[step % 2, index, a] = result[index]
        for side, edge in ((0, 7), (1, 0)):
            if a == edge:
                for place, index in enumerate(X_FACE[side]):
                    edges[step, 5 * side + place] = result[index]
            for place, index in enumerate(Y_FACE[side]):
                edges[step, 10 + 5 * side + place, a : a + 1, :] = result[index][edge : edge + 1, :]

    for step in range(STEPS):
        if step == 0:
            slice_step(step, 0)
            slice_step(step, 7)
            send_x(step)
            for a in range(1, 7):
                slice_step(step, a)
            send_y(step)
        else:
            whole(halos.at[step - 1, pl.ds(14, 10)], halo_recv.at[step - 1, 1])
            for a in range(1, 7):
                slice_step(step, a)
            whole(halos.at[step - 1, pl.ds(0, 14)], halo_recv.at[step - 1, 0])
            slice_step(step, 0)
            slice_step(step, 7)
            send_x(step)
            send_y(step)

    left = jnp.concatenate([part.astype(BF16) for part in parts_of(usum[...], STEP_PARTS)], axis=0)
    sub4 = sub[0:4]
    moved = []
    for k in range(GROUPS):
        if k % 2 == 0:
            picked = product(left, zhot[:, k * LANES : min(k + 2, GROUPS) * LANES], False)
            total = picked[0:96, :]
            for number in range(1, STEP_PARTS):
                total = total + picked[number * 96 : (number + 1) * 96, :]
        mask = rows32 == ((slots[k][0:1, :].astype(I32) >> 7) & 31)
        lanes = slice((k % 2) * LANES, (k % 2 + 1) * LANES)
        block = jnp.zeros((8, LANES), F32)
        for c in range(3):
            speed = jnp.sum(
                jnp.where(mask, total[c * 32 : (c + 1) * 32, lanes], 0.0), axis=0, keepdims=True
            )
            block = jnp.where(sub == c, speed, block)
        moved.append(block)
    tail = moved[TILES]
    for half in (1, 0):
        for dq in far_first:
            k = half * YZ + dq
            more = spread(jnp.where(lane_group == k, tail, 0.0))
            more = jnp.sum(jnp.where(own_group, more, 0.0), axis=0, keepdims=True)
            block = jnp.where(sub == 3, more, moved[k])[0:4, :]
            if k == 0:
                ret[0] = block
            else:
                back[k] = block
                pltpu.make_async_remote_copy(
                    src_ref=back.at[k],
                    dst_ref=ret.at[k],
                    send_sem=ret_send,
                    recv_sem=ret_recv,
                    device_id=device(-half, -dq),
                    device_id_type=MESH,
                ).start()

    last = STEPS - 1
    whole(halos.at[last, pl.ds(14, 10)], halo_recv.at[last, 1])
    whole(halos.at[last, pl.ds(0, 14)], halo_recv.at[last, 0])
    for a in range(8):
        for index in range(19):
            out_ref[index, a] = pulled(last, index, a)
    for step in range(STEPS):
        whole(halos.at[step], halo_send.at[step])
    whole(recv.at[pl.ds(1, TILES - 1), pl.ds(0, PUT_ROWS)], put_send)

    whole(ret.at[pl.ds(1, TILES - 1)], ret_recv)
    own4 = own_group[0:4]
    lefts = []
    for k in range(TILES):
        block = ret[k]
        more = jnp.where(own4, jnp.broadcast_to(block[3:4, :], (4, LANES)), 0.0)
        lefts.append(jnp.concatenate([block, more], axis=1))
    left = jnp.concatenate(lefts, axis=0)
    left = jnp.concatenate([part.astype(BF16) for part in parts_of(left, BIN_PARTS)], axis=0)
    taken = product(left, hot[...], False)
    rows = 4 * TILES
    total = taken[0:rows, :]
    for number in range(1, BIN_PARTS):
        total = total + taken[number * rows : (number + 1) * rows, :]
    final = None
    tile8 = jnp.broadcast_to(vals[6:7, :].astype(I32), (8, wide)) - (sub_wide >> 2)
    for pair in range(YZ):
        term = jnp.where(tile8 == 2 * pair, total[pair * 8 : (pair + 1) * 8, :], 0.0)
        final = term if final is None else final + term
    final = final[0:4, :] + final[4:8, :]
    dout_ref[...] = disp[...] + final[0:3, 0:marks]
    whole(ret.at[pl.ds(1, TILES - 1)], ret_send)


def body(populations, solid, displacement, stiffness, marker_tile, marker_site):
    marks = displacement.shape[1]
    wide = -(-marks // LANES) * LANES
    vmem = pl.BlockSpec(memory_space=pltpu.VMEM)
    hbm = pl.BlockSpec(memory_space=pltpu.HBM)
    dma = pltpu.SemaphoreType.DMA
    return pl.pallas_call(
        kernel,
        out_shape=(
            jax.ShapeDtypeStruct(populations.shape, F32),
            jax.ShapeDtypeStruct(displacement.shape, F32),
        ),
        in_specs=[hbm] * 6,
        out_specs=(vmem, vmem),
        scratch_shapes=[
            pltpu.VMEM(populations.shape, F32),
            pltpu.VMEM(solid.shape, I32),
            pltpu.VMEM(displacement.shape, F32),
            pltpu.VMEM((marks,), F32),
            pltpu.VMEM((1, marks), I32),
            pltpu.VMEM((marks,), I32),
            pltpu.VMEM((8, wide), F32),
            pltpu.VMEM((2 * LANES, wide), BF16),
            pltpu.VMEM((TILES, 8, LANES), F32),
            pltpu.VMEM((TILES, 8, LANES), F32),
            pltpu.VMEM((2 * LANES, SLOTS), BF16),
            pltpu.VMEM((128 * STEP_PARTS, SLOTS), BF16),
            pltpu.VMEM((96, 2 * LANES), F32),
            pltpu.VMEM((128, 2 * LANES), F32),
            pltpu.VMEM((GROUPS, 8, LANES), F32),
            pltpu.VMEM((2,) + populations.shape, F32),
            pltpu.VMEM((STEPS, 20, 8, LANES), F32),
            pltpu.VMEM((STEPS, 24, 8, LANES), F32),
            pltpu.VMEM((TILES, 4, LANES), F32),
            pltpu.VMEM((TILES, 4, LANES), F32),
            dma((6,)),
            dma,
            dma((2,)),
            dma,
            dma,
            dma((STEPS,)),
            dma((STEPS, 2)),
        ],
        compiler_params=pltpu.CompilerParams(
            collective_id=0, has_side_effects=True, vmem_limit_bytes=16 * 1024 * 1024
        ),
        name="lattice_steps",
    )(
        *(
            pltpu.with_memory_space_constraint(value, pltpu.HBM)
            for value in (
                populations,
                solid,
                displacement,
                stiffness,
                marker_tile.reshape(1, -1),
                marker_site,
            )
        )
    )


def solution(mesh):
    in_specs = (
        P(None, "gx", "yz", None),
        P("gx", "yz", None),
        P(None, ("gx", "yz")),
        P(("gx", "yz")),
        P(("gx", "yz"), None),
        P(("gx", "yz")),
    )
    out_specs = (P(None, "gx", "yz", None), P(None, ("gx", "yz")))
    return jax.shard_map(body, mesh=mesh, in_specs=in_specs, out_specs=out_specs, check_vma=False)
```

time: 49.7 us -> 43.7 us (0.88)
  local copies, waits for them, and re-layouts: 4.47 us -> 1.43 us
  Pallas kernels: 44.3 us -> 41.4 us
    pallas_call x1, Pallas kernels: 44.3 us -> 41.4 us  [body(): pl.pallas_call(kernel, out_shape=(jax.ShapeDtypeStruct(populations.shape,...]
    reshape x2 -> x0, local copies, waits for them, and re-layouts: 1.89 us -> none  [the longest x1 1.3 us: body(): stiffness.reshape(1, -1)]
    unnamed x6 -> x2, local copies, waits for them, and re-layouts: 2.58 us -> 1.43 us
where the time goes in v1:
time: 43.7 us; the launch traced here: 43.5 us
  Pallas kernels  41.4 us (95%)
  local copies, waits for them, and re-layouts  1.43 us (3%)
  between operations  0.64 us (1%)
    pallas_call x1, Pallas kernels, body(): pl.pallas_call(kernel, out_shape=(jax.ShapeDtypeStruct(populations.shape,...  41.4 us
    unnamed x2, local copies, waits for them, and re-layouts  1.43 us

profile of v1, /device:TPU:8, one launch (start us, length us, event | category | flops | bytes accessed | tf_op | source)
XLA Modules:
  0.0 43.5 jit_solution(9439232815264607180)
XLA Ops:
  0.6 41.4 %lattice_steps.1 = (f32[19,8,8,128]{3,2,1,0:T(8,128)S(1)}, f32[3,1088]{1,0:T(4,128)S(1)}) custom-call(f32[19,8,8,128]{3,2,1,0:T(8,128)} %pop_hbm.1, s32[8,8,128]{2,1,0:T(8,128)} %solid_hbm.1, f32[3,1088]{1,0:T(4,128)} %disp_hbm.1, f32[1088]{0:T(1024)} %stiff_hbm.1, s32[1,1088]{1,0:T(1,128)} %bitcast.1, s32[1088]{0:T(1024)} %site_hbm.1), custom_call_target="tpu_custom_call" | custom-call | tf_op jit(solution)/shard_map/lattice_steps/pallas_call | solution.py:438
  42.1 0.8 %copy.10 = f32[19,8,8,128]{3,2,1,0:T(8,128)} copy(f32[19,8,8,128]{3,2,1,0:T(8,128)S(1)} %get-tuple-element.4) | data formatting | bytes 1245184
  42.9 0.6 %copy.11 = f32[3,1088]{1,0:T(4,128)} copy(f32[3,1088]{1,0:T(4,128)S(1)} %get-tuple-element.5) | data formatting | bytes 26112

commit v2 on v1

--- a/solution.py
+++ b/solution.py
@@ -129,7 +129,7 @@
     pop_hbm, solid_hbm, disp_hbm, stiff_hbm, tile_hbm, site_hbm,
     out_ref, dout_ref,
     start, solid, disp, stiff, tile_in, site_in, vals, hot, payload, recv, zhot, lhs, usum, field, slots,
-    post, edges, halos, back, ret,
+    early, post, edges, halos, back, ret,
     load_sem, put_send, put_recv, ret_send, ret_recv, halo_send, halo_recv,
 ):
     marks = disp_hbm.shape[1]
@@ -147,7 +147,7 @@
     far_first = (4, 3, 5, 2, 6, 1, 7, 0)
     barrier = pltpu.get_barrier_semaphore()
     for dq in far_first:
-        for dg in (1, -1, 0):
+        for dg in (-1, 0):
             if (dg, dq) != (0, 0):
                 pl.semaphore_signal(barrier, inc=1, device_id=device(dg, dq), device_id_type=MESH)
 
@@ -216,7 +216,7 @@
         more = jnp.sum(jnp.where(own_group, more, 0.0), axis=0, keepdims=True)
         payload[k] = jnp.where(sub == 5, more, main)
 
-    pl.semaphore_wait(barrier, 3 * YZ - 1)
+    pl.semaphore_wait(barrier, 2 * YZ - 1)
 
     def whole(buffer, sem):
         pltpu.make_async_copy(buffer, buffer, sem).wait()
@@ -260,13 +260,15 @@
             more = jnp.where(own_group, jnp.broadcast_to(block[5:6, :], (8, LANES)), 0.0)
             tail = tail + jnp.where(lane_group == k, spread(more), 0.0)
             place_group(k, block)
-    slots[TILES] = tail
-    place_group(TILES, tail)
-    result = product(lhs[...], zhot[...], True)
-    total = result[0:128, :]
-    for number in range(1, STEP_PARTS):
-        total = total + result[number * 128 : (number + 1) * 128, :]
-    field[...] = total
+        if half == 1:
+            slots[TILES] = tail
+            place_group(TILES, tail)
+        lanes = slice(half * YZ * LANES, YZ * LANES if half == 0 else SLOTS)
+        result = product(lhs[:, lanes], zhot[:, lanes], True)
+        total = result[0:128, :]
+        for number in range(1, STEP_PARTS):
+            total = total + result[number * 128 : (number + 1) * 128, :]
+        field[...] = total if half == 0 else field[...] + total
     for load in loads[4:]:
         load.wait()
 
@@ -339,6 +341,28 @@
             for place, index in enumerate(Y_FACE[side]):
                 edges[step, 10 + 5 * side + place, a : a + 1, :] = result[index][edge : edge + 1, :]
 
+    def gather(lows):
+        rows = [usum[c * 32 + low : c * 32 + low + 8, :] for c in range(3) for low in lows]
+        count = 8 * len(rows)
+        left = jnp.concatenate(rows, axis=0)
+        left = jnp.concatenate([part.astype(BF16) for part in parts_of(left, STEP_PARTS)], axis=0)
+        for k in range(GROUPS):
+            if k % 2 == 0:
+                picked = product(left, zhot[:, k * LANES : min(k + 2, GROUPS) * LANES], False)
+                total = picked[0:count, :]
+                for number in range(1, STEP_PARTS):
+                    total = total + picked[number * count : (number + 1) * count, :]
+            row = (slots[k][0:1, :].astype(I32) >> 7) & 31
+            lanes = slice((k % 2) * LANES, (k % 2 + 1) * LANES)
+            masks = [sub + low == row for low in lows]
+            for c in range(3):
+                speed = None
+                for number, mask in enumerate(masks):
+                    top = (c * len(lows) + number) * 8
+                    term = jnp.where(mask, total[top : top + 8, lanes], 0.0)
+                    speed = term if speed is None else speed + term
+                yield k, c, speed
+
     for step in range(STEPS):
         if step == 0:
             slice_step(step, 0)
@@ -351,30 +375,21 @@
             whole(halos.at[step - 1, pl.ds(14, 10)], halo_recv.at[step - 1, 1])
             for a in range(1, 7):
                 slice_step(step, a)
+            if step == STEPS - 1:
+                for k, c, speed in gather((8, 16)):
+                    early[k, c] = speed
             whole(halos.at[step - 1, pl.ds(0, 14)], halo_recv.at[step - 1, 0])
             slice_step(step, 0)
             slice_step(step, 7)
             send_x(step)
             send_y(step)
 
-    left = jnp.concatenate([part.astype(BF16) for part in parts_of(usum[...], STEP_PARTS)], axis=0)
-    sub4 = sub[0:4]
     moved = []
-    for k in range(GROUPS):
-        if k % 2 == 0:
-            picked = product(left, zhot[:, k * LANES : min(k + 2, GROUPS) * LANES], False)
-            total = picked[0:96, :]
-            for number in range(1, STEP_PARTS):
-                total = total + picked[number * 96 : (number + 1) * 96, :]
-        mask = rows32 == ((slots[k][0:1, :].astype(I32) >> 7) & 31)
-        lanes = slice((k % 2) * LANES, (k % 2 + 1) * LANES)
-        block = jnp.zeros((8, LANES), F32)
-        for c in range(3):
-            speed = jnp.sum(
-                jnp.where(mask, total[c * 32 : (c + 1) * 32, lanes], 0.0), axis=0, keepdims=True
-            )
-            block = jnp.where(sub == c, speed, block)
-        moved.append(block)
+    for k, c, speed in gather((0, 24)):
+        speed = jnp.sum(speed + early[k, c], axis=0, keepdims=True)
+        if c == 0:
+            moved.append(jnp.zeros((8, LANES), F32))
+        moved[k] = jnp.where(sub == c, speed, moved[k])
     tail = moved[TILES]
     for half in (1, 0):
         for dq in far_first:
@@ -397,8 +412,11 @@
 
     last = STEPS - 1
     whole(halos.at[last, pl.ds(14, 10)], halo_recv.at[last, 1])
+    for a in range(1, 7):
+        for index in range(19):
+            out_ref[index, a] = pulled(last, index, a)
     whole(halos.at[last, pl.ds(0, 14)], halo_recv.at[last, 0])
-    for a in range(8):
+    for a in (0, 7):
         for index in range(19):
             out_ref[index, a] = pulled(last, index, a)
     for step in range(STEPS):
@@ -429,13 +447,25 @@
     whole(ret.at[pl.ds(1, TILES - 1)], ret_send)
 
 
+def flush(pop_ref, disp_ref, pop_hbm, disp_hbm, sems):
+    copies = [pltpu.make_async_copy(disp_ref, disp_hbm, sems.at[0])]
+    step = 4
+    for number, first in enumerate(range(0, pop_ref.shape[0], step)):
+        part = pl.ds(first, min(step, pop_ref.shape[0] - first))
+        copies.append(pltpu.make_async_copy(pop_ref.at[part], pop_hbm.at[part], sems.at[number + 1]))
+    for copy in copies:
+        copy.start()
+    for copy in copies:
+        copy.wait()
+
+
 def body(populations, solid, displacement, stiffness, marker_tile, marker_site):
     marks = displacement.shape[1]
     wide = -(-marks // LANES) * LANES
     vmem = pl.BlockSpec(memory_space=pltpu.VMEM)
     hbm = pl.BlockSpec(memory_space=pltpu.HBM)
     dma = pltpu.SemaphoreType.DMA
-    return pl.pallas_call(
+    final_pop, final_disp = pl.pallas_call(
         kernel,
         out_shape=(
             jax.ShapeDtypeStruct(populations.shape, F32),
@@ -459,6 +489,7 @@
             pltpu.VMEM((96, 2 * LANES), F32),
             pltpu.VMEM((128, 2 * LANES), F32),
             pltpu.VMEM((GROUPS, 8, LANES), F32),
+            pltpu.VMEM((GROUPS, 3, 8, LANES), F32),
             pltpu.VMEM((2,) + populations.shape, F32),
             pltpu.VMEM((STEPS, 20, 8, LANES), F32),
             pltpu.VMEM((STEPS, 24, 8, LANES), F32),
@@ -489,6 +520,18 @@
             )
         )
     )
+    return pl.pallas_call(
+        flush,
+        out_shape=(
+            jax.ShapeDtypeStruct(populations.shape, F32),
+            jax.ShapeDtypeStruct(displacement.shape, F32),
+        ),
+        in_specs=[vmem, vmem],
+        out_specs=(hbm, hbm),
+        scratch_shapes=[dma((6,))],
+        compiler_params=pltpu.CompilerParams(vmem_limit_bytes=16 * 1024 * 1024),
+        name="write_out",
+    )(final_pop, final_disp)
 
 
 def solution(mesh):

time: 43.7 us -> 41.4 us (0.947)
  local copies, waits for them, and re-layouts: 1.43 us -> 0 us
  Pallas kernels: 41.4 us -> 40.6 us
    pallas_call x1, Pallas kernels: 41.4 us -> 39.8 us  [body(): pl.pallas_call(kernel, out_shape=(jax.ShapeDtypeStruct(populations.shape,...]
    unnamed x2 -> x0, local copies, waits for them, and re-layouts: 1.43 us -> none
    pallas_call x0 -> x1, Pallas kernels: none -> 0.87 us  [body(): pl.pallas_call(flush, out_shape=(jax.ShapeDtypeStruct(populations.shape,...]
where the time goes in v2:
time: 41.4 us; the launch traced here: 41.3 us
  Pallas kernels  40.6 us (98%)
  between operations  0.64 us (2%)
    pallas_call x1, Pallas kernels, body(): pl.pallas_call(kernel, out_shape=(jax.ShapeDtypeStruct(populations.shape,...  39.8 us
    pallas_call x1, Pallas kernels, body(): pl.pallas_call(flush, out_shape=(jax.ShapeDtypeStruct(populations.shape,...  0.87 us

profile of v2, /device:TPU:8, one launch (start us, length us, event | category | flops | bytes accessed | tf_op | source)
XLA Modules:
  0.0 41.3 jit_solution(8180840441900961060)
XLA Ops:
  0.6 39.8 %lattice_steps.1 = (f32[19,8,8,128]{3,2,1,0:T(8,128)S(1)}, f32[3,1088]{1,0:T(4,128)S(1)}) custom-call(f32[19,8,8,128]{3,2,1,0:T(8,128)} %pop_hbm.1, s32[8,8,128]{2,1,0:T(8,128)} %solid_hbm.1, f32[3,1088]{1,0:T(4,128)} %disp_hbm.1, f32[1088]{0:T(1024)} %stiff_hbm.1, s32[1,1088]{1,0:T(1,128)} %bitcast.1, s32[1088]{0:T(1024)} %site_hbm.1), custom_call_target="tpu_custom_call" | custom-call | tf_op jit(solution)/shard_map/lattice_steps/pallas_call | solution.py:468
  40.4 0.9 %write_out.1 = (f32[19,8,8,128]{3,2,1,0:T(8,128)}, f32[3,1088]{1,0:T(4,128)}) custom-call(f32[19,8,8,128]{3,2,1,0:T(8,128)S(1)} %get-tuple-element.4.pop_ref, f32[3,1088]{1,0:T(4,128)S(1)} %get-tuple-element.5.disp_ref), custom_call_target="tpu_custom_call" | custom-call | tf_op jit(solution)/shard_map/write_out/pallas_call | solution.py:523

commit v3 on v2

--- a/solution.py
+++ b/solution.py
@@ -8,7 +8,6 @@
 from jax.sharding import PartitionSpec as P
 
 MESH = pl.DeviceIdType.MESH
-STEPS = 3
 F32 = jnp.float32
 BF16 = jnp.bfloat16
 I32 = jnp.int32
@@ -129,7 +128,7 @@
     pop_hbm, solid_hbm, disp_hbm, stiff_hbm, tile_hbm, site_hbm,
     out_ref, dout_ref,
     start, solid, disp, stiff, tile_in, site_in, vals, hot, payload, recv, zhot, lhs, usum, field, slots,
-    early, post, edges, halos, back, ret,
+    main, skirt, main_next, skirt_next, post, edges, halos, back, ret,
     load_sem, put_send, put_recv, ret_send, ret_recv, halo_send, halo_recv,
 ):
     marks = disp_hbm.shape[1]
@@ -211,10 +210,10 @@
         term = product(left.astype(BF16), hot[...], True)
         binned = term if binned is None else binned + term
     for k in range(TILES):
-        main = binned[k * 8 : (k + 1) * 8, 0:LANES]
+        low_ranks = binned[k * 8 : (k + 1) * 8, 0:LANES]
         more = binned[k * 8 : (k + 1) * 8, LANES : 2 * LANES]
         more = jnp.sum(jnp.where(own_group, more, 0.0), axis=0, keepdims=True)
-        payload[k] = jnp.where(sub == 5, more, main)
+        payload[k] = jnp.where(sub == 5, more, low_ranks)
 
     pl.semaphore_wait(barrier, 2 * YZ - 1)
 
@@ -272,121 +271,187 @@
     for load in loads[4:]:
         load.wait()
 
-    def pulled(step, index, a):
-        cx, cy, cz = lattice_dirs[index]
+    def streamed(index, main, skirt):
+        _, cy, cz = lattice_dirs[index]
+        value = main
+        if cy != 0:
+            value = jnp.where(sub == (7 if cy > 0 else 0), skirt, main)
+            value = pltpu.roll(value, cy % 8, 0)
+        if cz != 0:
+            value = pltpu.roll(value, cz % LANES, 1)
+        return value
+
+    def remote(src, dst, send, recv_of, dg, dq):
+        pltpu.make_async_remote_copy(
+            src_ref=src,
+            dst_ref=dst,
+            send_sem=send,
+            recv_sem=recv_of,
+            device_id=device(dg, dq),
+            device_id_type=MESH,
+        ).start()
+
+    def margin(channels, ax, ay, dg, dq, which):
+        first, count = channels
+        part = pl.ds(first, count)
+        a_src, a_dst = {0: (2, 2), 1: (10 - ax, 2 - ax), -1: (2, 10)}[dg]
+        slices = ax if dg != 0 else 8
+        b_src = {0: 0, 1: 8 - ay, -1: 0}[dq]
+        rows = pl.ds(b_src, ay if dq != 0 else 8)
+        into = main if dq == 0 else skirt
+        remote(
+            main.at[part, pl.ds(a_src, slices), rows],
+            into.at[part, pl.ds(a_dst, slices), rows],
+            halo_send.at[0, which],
+            halo_recv.at[0, which],
+            dg,
+            dq,
+        )
+
+    def margin_x():
+        for index in CORNER:
+            dg, dq, _ = lattice_dirs[index]
+            margin((index, 1), 2, 2, dg, dq, 0)
+            margin((0, 7), 2, 2, dg, dq, 0)
+            margin((11, 4), 2, 1, dg, dq, 0)
+            margin((15, 4), 1, 2, dg, dq, 0)
+            margin((19, 4), 1, 1, dg, dq, 0)
+        for side, dg in ((0, 1), (1, -1)):
+            for index in X_FACE[side]:
+                margin((index, 1), 2, 0, dg, 0, 0)
+            for channels in ((0, 1), (3, 4), (15, 8)):
+                margin(channels, 1, 0, dg, 0, 0)
+
+    def margin_y():
+        for side, dq in ((0, 1), (1, -1)):
+            for index in Y_FACE[side]:
+                margin((index, 1), 0, 2, 0, dq, 1)
+            for channels in ((0, 3), (5, 2), (11, 4), (19, 4)):
+                margin(channels, 0, 1, 0, dq, 1)
+
+    def span(a):
+        low = (a % 4) * 8
+        high = (a // 4) * LANES
+        return [(slice(c * 32 + low, c * 32 + low + 8), slice(high, high + LANES)) for c in range(4)]
+
+    def first_step(a):
+        spans = span(a)
+        stiff_sum, *forces = [field[place] for place in spans]
+        result, speed = collide([start[index, a] for index in range(19)], forces, solid[a])
+        for index in range(19):
+            main[index, a + 2] = result[index]
+        for c in range(3):
+            usum[spans[c]] = speed[c]
+            main[19 + c, a + 2] = forces[c] - stiff_sum * speed[c]
+        main[22, a + 2] = solid[a].astype(F32)
+
+    def second_step(a, outside):
+        own, other = (skirt, main) if outside else (main, skirt)
+        popul = []
+        for index in range(19):
+            source = a - lattice_dirs[index][0] + 2
+            popul.append(streamed(index, own[index, source], other[index, source]))
+        forces = [own[19 + c, a + 2] for c in range(3)]
+        result, speed = collide(popul, forces, own[22, a + 2])
+        for index in range(19):
+            (skirt_next if outside else main_next)[index, a + 1] = result[index]
+        if not outside and 0 <= a < 8:
+            spans = span(a)
+            stiff_sum = field[spans[0]]
+            for c in range(3):
+                usum[spans[c]] = usum[spans[c]] + speed[c]
+                field[spans[c + 1]] = forces[c] - stiff_sum * speed[c]
+
+    def third_step(a):
+        popul = []
+        for index in range(19):
+            source = a - lattice_dirs[index][0] + 1
+            popul.append(streamed(index, main_next[index, source], skirt_next[index, source]))
+        spans = span(a)
+        result, speed = collide(popul, [field[place] for place in spans[1:]], solid[a])
+        for c in range(3):
+            usum[spans[c]] = usum[spans[c]] + speed[c]
+        for index in range(19):
+            post[index, a] = result[index]
+        for side, edge in ((0, 7), (1, 0)):
+            if a == edge:
+                for place, index in enumerate(X_FACE[side]):
+                    edges[5 * side + place] = result[index]
+            for place, index in enumerate(Y_FACE[side]):
+                edges[10 + 5 * side + place, a : a + 1, :] = result[index][edge : edge + 1, :]
+
+    def halo(src, first, count, dg, dq):
+        which = 0 if first < 14 else 1
+        remote(
+            edges.at[pl.ds(src, count)],
+            halos.at[pl.ds(first, count)],
+            halo_send.at[1, which],
+            halo_recv.at[1, which],
+            dg,
+            dq,
+        )
+
+    def pulled(index, a):
+        cx, cy, _ = lattice_dirs[index]
         x_side = 0 if cx > 0 else 1
         y_side = 0 if cy > 0 else 1
         source = a - cx
         inside = 0 <= source < 8
-        if inside:
-            value = post[step % 2, index, source]
-        else:
-            value = halos[step, 5 * x_side + X_FACE[x_side].index(index)]
+        value = post[index, source] if inside else halos[5 * x_side + X_FACE[x_side].index(index)]
+        other = value
         if cy != 0:
             if inside:
-                tile_of = 10 + 4 + 5 * y_side + Y_FACE[y_side].index(index)
-                other = jnp.broadcast_to(halos[step, tile_of, source : source + 1, :], (8, LANES))
+                tile_of = 14 + 5 * y_side + Y_FACE[y_side].index(index)
+                other = jnp.broadcast_to(halos[tile_of, source : source + 1, :], (8, LANES))
             else:
-                other = halos[step, 10 + CORNER.index(index)]
-            value = jnp.where(sub == (7 if cy > 0 else 0), other, value)
-            value = pltpu.roll(value, cy % 8, 0)
-        if cz != 0:
-            value = pltpu.roll(value, cz % LANES, 1)
-        return value
-
-    def halo(step, src, first, count, dg, dq):
-        pltpu.make_async_remote_copy(
-            src_ref=edges.at[step, pl.ds(src, count)],
-            dst_ref=halos.at[step, pl.ds(first, count)],
-            send_sem=halo_send.at[step],
-            recv_sem=halo_recv.at[step, 0 if first < 14 else 1],
-            device_id=device(dg, dq),
-            device_id_type=MESH,
-        ).start()
-
-    def send_x(step):
-        for number, index in enumerate(CORNER):
-            cx, cy, _ = lattice_dirs[index]
-            side = 0 if cx > 0 else 1
-            halo(step, 5 * side + X_FACE[side].index(index), 10 + number, 1, cx, cy)
-        for side, dg in ((0, 1), (1, -1)):
-            halo(step, 5 * side, 5 * side, 5, dg, 0)
-
-    def send_y(step):
-        for side, dq in ((0, 1), (1, -1)):
-            halo(step, 10 + 5 * side, 14 + 5 * side, 5, 0, dq)
-
-    def slice_step(step, a):
-        if step == 0:
-            popul = [start[index, a] for index in range(19)]
-        else:
-            popul = [pulled(step - 1, index, a) for index in range(19)]
-        low = (a % 4) * 8
-        high = (a // 4) * LANES
-        stiff_sum, *forces = [field[c * 32 + low : c * 32 + low + 8, high : high + LANES] for c in range(4)]
-        result, speed = collide(popul, forces, solid[a])
-        for c in range(3):
-            place = (slice(c * 32 + low, c * 32 + low + 8), slice(high, high + LANES))
-            usum[place] = speed[c] if step == 0 else usum[place] + speed[c]
-            if step < STEPS - 1:
-                field[32 + c * 32 + low : 32 + c * 32 + low + 8, high : high + LANES] = (
-                    forces[c] - stiff_sum * speed[c]
-                )
-        for index in range(19):
-            post[step % 2, index, a] = result[index]
-        for side, edge in ((0, 7), (1, 0)):
-            if a == edge:
-                for place, index in enumerate(X_FACE[side]):
-                    edges[step, 5 * side + place] = result[index]
-            for place, index in enumerate(Y_FACE[side]):
-                edges[step, 10 + 5 * side + place, a : a + 1, :] = result[index][edge : edge + 1, :]
-
-    def gather(lows):
-        rows = [usum[c * 32 + low : c * 32 + low + 8, :] for c in range(3) for low in lows]
-        count = 8 * len(rows)
-        left = jnp.concatenate(rows, axis=0)
-        left = jnp.concatenate([part.astype(BF16) for part in parts_of(left, STEP_PARTS)], axis=0)
+                other = halos[10 + CORNER.index(index)]
+        return streamed(index, value, other)
+
+    def gather():
+        left = jnp.concatenate([part.astype(BF16) for part in parts_of(usum[...], STEP_PARTS)], axis=0)
         for k in range(GROUPS):
             if k % 2 == 0:
                 picked = product(left, zhot[:, k * LANES : min(k + 2, GROUPS) * LANES], False)
-                total = picked[0:count, :]
+                total = picked[0:96, :]
                 for number in range(1, STEP_PARTS):
-                    total = total + picked[number * count : (number + 1) * count, :]
-            row = (slots[k][0:1, :].astype(I32) >> 7) & 31
+                    total = total + picked[number * 96 : (number + 1) * 96, :]
+            mask = rows32 == ((slots[k][0:1, :].astype(I32) >> 7) & 31)
             lanes = slice((k % 2) * LANES, (k % 2 + 1) * LANES)
-            masks = [sub + low == row for low in lows]
             for c in range(3):
-                speed = None
-                for number, mask in enumerate(masks):
-                    top = (c * len(lows) + number) * 8
-                    term = jnp.where(mask, total[top : top + 8, lanes], 0.0)
-                    speed = term if speed is None else speed + term
-                yield k, c, speed
-
-    for step in range(STEPS):
-        if step == 0:
-            slice_step(step, 0)
-            slice_step(step, 7)
-            send_x(step)
-            for a in range(1, 7):
-                slice_step(step, a)
-            send_y(step)
-        else:
-            whole(halos.at[step - 1, pl.ds(14, 10)], halo_recv.at[step - 1, 1])
-            for a in range(1, 7):
-                slice_step(step, a)
-            if step == STEPS - 1:
-                for k, c, speed in gather((8, 16)):
-                    early[k, c] = speed
-            whole(halos.at[step - 1, pl.ds(0, 14)], halo_recv.at[step - 1, 0])
-            slice_step(step, 0)
-            slice_step(step, 7)
-            send_x(step)
-            send_y(step)
+                speed = jnp.where(mask, total[c * 32 : (c + 1) * 32, lanes], 0.0)
+                yield k, c, jnp.sum(speed, axis=0, keepdims=True)
+
+    for a in (0, 1, 6, 7):
+        first_step(a)
+    margin_x()
+    for a in range(2, 6):
+        first_step(a)
+    margin_y()
+    whole(main.at[:, pl.ds(0, 2)], halo_recv.at[0, 1])
+    for a in range(1, 7):
+        second_step(a, False)
+        second_step(a, True)
+    for a in range(2, 6):
+        third_step(a)
+    whole(main.at[pl.ds(0, 6)], halo_recv.at[0, 0])
+    for a in (-1, 0, 7, 8):
+        second_step(a, False)
+        second_step(a, True)
+    third_step(0)
+    third_step(7)
+    for number, index in enumerate(CORNER):
+        cx, cy, _ = lattice_dirs[index]
+        side = 0 if cx > 0 else 1
+        halo(5 * side + X_FACE[side].index(index), 10 + number, 1, cx, cy)
+    for side, dg in ((0, 1), (1, -1)):
+        halo(5 * side, 5 * side, 5, dg, 0)
+    third_step(1)
+    third_step(6)
+    for side, dq in ((0, 1), (1, -1)):
+        halo(10 + 5 * side, 14 + 5 * side, 5, 0, dq)
 
     moved = []
-    for k, c, speed in gather((0, 24)):
-        speed = jnp.sum(speed + early[k, c], axis=0, keepdims=True)
+    for k, c, speed in gather():
         if c == 0:
             moved.append(jnp.zeros((8, LANES), F32))
         moved[k] = jnp.where(sub == c, speed, moved[k])
@@ -410,17 +475,18 @@
                     device_id_type=MESH,
                 ).start()
 
-    last = STEPS - 1
-    whole(halos.at[last, pl.ds(14, 10)], halo_recv.at[last, 1])
+    whole(halos.at[pl.ds(14, 10)], halo_recv.at[1, 1])
     for a in range(1, 7):
         for index in range(19):
-            out_ref[index, a] = pulled(last, index, a)
-    whole(halos.at[last, pl.ds(0, 14)], halo_recv.at[last, 0])
+            out_ref[index, a] = pulled(index, a)
+    whole(halos.at[pl.ds(0, 14)], halo_recv.at[1, 0])
     for a in (0, 7):
         for index in range(19):
-            out_ref[index, a] = pulled(last, index, a)
-    for step in range(STEPS):
-        whole(halos.at[step], halo_send.at[step])
+            out_ref[index, a] = pulled(index, a)
+    whole(main.at[pl.ds(0, 6)], halo_send.at[0, 0])
+    whole(main.at[:, pl.ds(0, 2)], halo_send.at[0, 1])
+    whole(halos.at[pl.ds(0, 14)], halo_send.at[1, 0])
+    whole(halos.at[pl.ds(14, 10)], halo_send.at[1, 1])
     whole(recv.at[pl.ds(1, TILES - 1), pl.ds(0, PUT_ROWS)], put_send)
 
     whole(ret.at[pl.ds(1, TILES - 1)], ret_recv)
@@ -489,10 +555,13 @@
             pltpu.VMEM((96, 2 * LANES), F32),
             pltpu.VMEM((128, 2 * LANES), F32),
             pltpu.VMEM((GROUPS, 8, LANES), F32),
-            pltpu.VMEM((GROUPS, 3, 8, LANES), F32),
-            pltpu.VMEM((2,) + populations.shape, F32),
-            pltpu.VMEM((STEPS, 20, 8, LANES), F32),
-            pltpu.VMEM((STEPS, 24, 8, LANES), F32),
+            pltpu.VMEM((23, 12, 8, LANES), F32),
+            pltpu.VMEM((23, 12, 8, LANES), F32),
+            pltpu.VMEM((19, 10, 8, LANES), F32),
+            pltpu.VMEM((19, 10, 8, LANES), F32),
+            pltpu.VMEM(populations.shape, F32),
+            pltpu.VMEM((20, 8, LANES), F32),
+            pltpu.VMEM((24, 8, LANES), F32),
             pltpu.VMEM((TILES, 4, LANES), F32),
             pltpu.VMEM((TILES, 4, LANES), F32),
             dma((6,)),
@@ -500,8 +569,8 @@
             dma((2,)),
             dma,
             dma,
-            dma((STEPS,)),
-            dma((STEPS, 2)),
+            dma((2, 2)),
+            dma((2, 2)),
         ],
         compiler_params=pltpu.CompilerParams(
             collective_id=0, has_side_effects=True, vmem_limit_bytes=16 * 1024 * 1024

time: 41.4 us -> 36.9 us (0.89)
  Pallas kernels: 40.6 us -> 36.1 us
    pallas_call x1, Pallas kernels: 39.8 us -> 35.2 us  [body(): pl.pallas_call(kernel, out_shape=(jax.ShapeDtypeStruct(populations.shape,...]
where the time goes in v3:
time: 36.9 us; the launch traced here: 36.7 us
  Pallas kernels  36.1 us (98%)
  between operations  0.64 us (2%)
    pallas_call x1, Pallas kernels, body(): pl.pallas_call(kernel, out_shape=(jax.ShapeDtypeStruct(populations.shape,...  35.2 us
    pallas_call x1, Pallas kernels, body(): pl.pallas_call(flush, out_shape=(jax.ShapeDtypeStruct(populations.shape,...  0.87 us

profile of v3, /device:TPU:8, one launch (start us, length us, event | category | flops | bytes accessed | tf_op | source)
XLA Modules:
  0.0 36.7 jit_solution(15122230751331533124)
XLA Ops:
  0.6 35.2 %lattice_steps.1 = (f32[19,8,8,128]{3,2,1,0:T(8,128)S(1)}, f32[3,1088]{1,0:T(4,128)S(1)}) custom-call(f32[19,8,8,128]{3,2,1,0:T(8,128)} %pop_hbm.1, s32[8,8,128]{2,1,0:T(8,128)} %solid_hbm.1, f32[3,1088]{1,0:T(4,128)} %disp_hbm.1, f32[1088]{0:T(1024)} %stiff_hbm.1, s32[1,1088]{1,0:T(1,128)} %bitcast.1, s32[1088]{0:T(1024)} %site_hbm.1), custom_call_target="tpu_custom_call" | custom-call | tf_op jit(solution)/shard_map/lattice_steps/pallas_call | solution.py:534
  35.8 0.9 %write_out.1 = (f32[19,8,8,128]{3,2,1,0:T(8,128)}, f32[3,1088]{1,0:T(4,128)}) custom-call(f32[19,8,8,128]{3,2,1,0:T(8,128)S(1)} %get-tuple-element.4.pop_ref, f32[3,1088]{1,0:T(4,128)S(1)} %get-tuple-element.5.disp_ref), custom_call_target="tpu_custom_call" | custom-call | tf_op jit(solution)/shard_map/write_out/pallas_call | solution.py:592

commit v4 on v3

--- a/solution.py
+++ b/solution.py
@@ -40,6 +40,14 @@
 X_FACE = [[1, 7, 9, 11, 13], [2, 8, 10, 12, 14]]
 Y_FACE = [[3, 7, 10, 15, 17], [4, 8, 9, 16, 18]]
 CORNER = [7, 8, 9, 10]
+
+CHANNELS = [7, 1, 11, 13, 9, 3, 15, 17, 0, 5, 6, 19, 20, 21, 22, 4, 16, 18, 10, 2, 12, 14, 8]
+SPOT = {channel: place for place, channel in enumerate(CHANNELS)}
+RUNS = {
+    (1, 1): (0, 1), (1, 0): (1, 3), (1, -1): (4, 1),
+    (0, 1): (5, 3), (0, 0): (8, 7), (0, -1): (15, 3),
+    (-1, 1): (18, 1), (-1, 0): (19, 3), (-1, -1): (22, 1),
+}
 
 YZ = 8
 TILES = 2 * YZ
@@ -233,21 +241,31 @@
                     device_id_type=MESH,
                 ).start()
 
-    rows32 = iota((32, LANES), 0)
+    lane_rows = [(iota((16, LANES), 0) + top).astype(F32).astype(BF16) for top in range(0, 2 * LANES, 16)]
+    one = jnp.ones((16, LANES), BF16)
+    zero = jnp.zeros((16, LANES), BF16)
+
+    def row_of(site):
+        return ((site >> 7) & 31) ^ ((site >> 12) * 24)
+
+    def packed(row):
+        return jnp.broadcast_to(row, (16, LANES)).astype(BF16)
+
 
     def place_group(k, block):
         site = block[0:1, :].astype(I32)
-        place = ((site >> 12) << 7) + (site & 127)
-        zhot[:, k * LANES : (k + 1) * LANES] = jnp.where(
-            iota((2 * LANES, LANES), 0) == place, 1.0, 0.0
-        ).astype(BF16)
-        mask = rows32 == ((site >> 7) & 31)
+        place = packed((((site >> 12) << 7) + (site & 127)).astype(F32))
+        lanes = slice(k * LANES, (k + 1) * LANES)
+        for number, index in enumerate(lane_rows):
+            zhot[number * 16 : (number + 1) * 16, lanes] = jnp.where(index == place, one, zero)
+        row = packed(row_of(site).astype(F32))
+        masks = [lane_rows[number] == row for number in range(2)]
         for number, part in enumerate(parts_of(block, STEP_PARTS)):
             for c in range(4):
                 top = (number * 4 + c) * 32
-                lhs[top : top + 32, k * LANES : (k + 1) * LANES] = jnp.where(
-                    mask, part[1 + c : 2 + c, :], 0.0
-                ).astype(BF16)
+                value = packed(part[1 + c : 2 + c, :])
+                for below, mask in enumerate(masks):
+                    lhs[top + below * 16 : top + (below + 1) * 16, lanes] = jnp.where(mask, value, zero)
 
     tail = jnp.zeros((8, LANES), F32)
     for half in range(2):
@@ -309,28 +327,23 @@
         )
 
     def margin_x():
-        for index in CORNER:
-            dg, dq, _ = lattice_dirs[index]
-            margin((index, 1), 2, 2, dg, dq, 0)
-            margin((0, 7), 2, 2, dg, dq, 0)
-            margin((11, 4), 2, 1, dg, dq, 0)
-            margin((15, 4), 1, 2, dg, dq, 0)
-            margin((19, 4), 1, 1, dg, dq, 0)
-        for side, dg in ((0, 1), (1, -1)):
-            for index in X_FACE[side]:
-                margin((index, 1), 2, 0, dg, 0, 0)
-            for channels in ((0, 1), (3, 4), (15, 8)):
-                margin(channels, 1, 0, dg, 0, 0)
+        for dg, dq in ((1, 1), (-1, -1), (1, -1), (-1, 1)):
+            margin(RUNS[dg, dq], 2, 2, dg, dq, 0)
+            margin(RUNS[dg, 0], 2, 1, dg, dq, 0)
+            margin(RUNS[0, dq], 1, 2, dg, dq, 0)
+            margin(RUNS[0, 0], 1, 1, dg, dq, 0)
+        for dg in (1, -1):
+            margin((0 if dg > 0 else 18, 5), 2, 0, dg, 0, 0)
+            margin((5, 13), 1, 0, dg, 0, 0)
 
     def margin_y():
-        for side, dq in ((0, 1), (1, -1)):
-            for index in Y_FACE[side]:
-                margin((index, 1), 0, 2, 0, dq, 1)
-            for channels in ((0, 3), (5, 2), (11, 4), (19, 4)):
-                margin(channels, 0, 1, 0, dq, 1)
+        for dq in (1, -1):
+            for cx in (1, 0, -1):
+                margin(RUNS[cx, dq], 0, 2, 0, dq, 1)
+                margin(RUNS[cx, 0], 0, 1, 0, dq, 1)
 
     def span(a):
-        low = (a % 4) * 8
+        low = min(a, 7 - a) * 8
         high = (a // 4) * LANES
         return [(slice(c * 32 + low, c * 32 + low + 8), slice(high, high + LANES)) for c in range(4)]
 
@@ -339,22 +352,26 @@
         stiff_sum, *forces = [field[place] for place in spans]
         result, speed = collide([start[index, a] for index in range(19)], forces, solid[a])
         for index in range(19):
-            main[index, a + 2] = result[index]
+            main[SPOT[index], a + 2] = result[index]
         for c in range(3):
             usum[spans[c]] = speed[c]
-            main[19 + c, a + 2] = forces[c] - stiff_sum * speed[c]
-        main[22, a + 2] = solid[a].astype(F32)
+            main[SPOT[19 + c], a + 2] = forces[c] - stiff_sum * speed[c]
+        main[SPOT[22], a + 2] = solid[a].astype(F32)
 
     def second_step(a, outside):
         own, other = (skirt, main) if outside else (main, skirt)
         popul = []
         for index in range(19):
             source = a - lattice_dirs[index][0] + 2
-            popul.append(streamed(index, own[index, source], other[index, source]))
-        forces = [own[19 + c, a + 2] for c in range(3)]
-        result, speed = collide(popul, forces, own[22, a + 2])
+            spot = SPOT[index]
+            popul.append(streamed(index, own[spot, source], other[spot, source]))
+        forces = [own[SPOT[19 + c], a + 2] for c in range(3)]
+        result, speed = collide(popul, forces, own[SPOT[22], a + 2])
         for index in range(19):
-            (skirt_next if outside else main_next)[index, a + 1] = result[index]
+            cx, cy, _ = lattice_dirs[index]
+            enters = cx == 1 if a < 0 else cx == -1 if a > 7 else True
+            if enters and (cy != 0 or not outside):
+                (skirt_next if outside else main_next)[index, a + 1] = result[index]
         if not outside and 0 <= a < 8:
             spans = span(a)
             stiff_sum = field[spans[0]]
@@ -415,7 +432,7 @@
                 total = picked[0:96, :]
                 for number in range(1, STEP_PARTS):
                     total = total + picked[number * 96 : (number + 1) * 96, :]
-            mask = rows32 == ((slots[k][0:1, :].astype(I32) >> 7) & 31)
+            mask = iota((32, LANES), 0) == row_of(slots[k][0:1, :].astype(I32))
             lanes = slice((k % 2) * LANES, (k % 2 + 1) * LANES)
             for c in range(3):
                 speed = jnp.where(mask, total[c * 32 : (c + 1) * 32, lanes], 0.0)
@@ -433,7 +450,7 @@
         second_step(a, True)
     for a in range(2, 6):
         third_step(a)
-    whole(main.at[pl.ds(0, 6)], halo_recv.at[0, 0])
+    whole(main.at[:, pl.ds(0, 5), pl.ds(0, 4)], halo_recv.at[0, 0])
     for a in (-1, 0, 7, 8):
         second_step(a, False)
         second_step(a, True)
@@ -483,7 +500,7 @@
     for a in (0, 7):
         for index in range(19):
             out_ref[index, a] = pulled(index, a)
-    whole(main.at[pl.ds(0, 6)], halo_send.at[0, 0])
+    whole(main.at[:, pl.ds(0, 5), pl.ds(0, 4)], halo_send.at[0, 0])
     whole(main.at[:, pl.ds(0, 2)], halo_send.at[0, 1])
     whole(halos.at[pl.ds(0, 14)], halo_send.at[1, 0])
     whole(halos.at[pl.ds(14, 10)], halo_send.at[1, 1])

time: 36.9 us -> 36.7 us (level)
  no operation moved by 1% of the time
where the time goes in v4:
time: 36.7 us; the launch traced here: 36.6 us
  Pallas kernels  35.9 us (98%)
  between operations  0.64 us (2%)
    pallas_call x1, Pallas kernels, body(): pl.pallas_call(kernel, out_shape=(jax.ShapeDtypeStruct(populations.shape,...  35 us
    pallas_call x1, Pallas kernels, body(): pl.pallas_call(flush, out_shape=(jax.ShapeDtypeStruct(populations.shape,...  0.87 us

profile of v4, /device:TPU:8, one launch (start us, length us, event | category | flops | bytes accessed | tf_op | source)
XLA Modules:
  0.0 36.6 jit_solution(7987246315539614724)
XLA Ops:
  0.6 35.0 %lattice_steps.1 = (f32[19,8,8,128]{3,2,1,0:T(8,128)S(1)}, f32[3,1088]{1,0:T(4,128)S(1)}) custom-call(f32[19,8,8,128]{3,2,1,0:T(8,128)} %pop_hbm.1, s32[8,8,128]{2,1,0:T(8,128)} %solid_hbm.1, f32[3,1088]{1,0:T(4,128)} %disp_hbm.1, f32[1088]{0:T(1024)} %stiff_hbm.1, s32[1,1088]{1,0:T(1,128)} %bitcast.1, s32[1088]{0:T(1024)} %site_hbm.1), custom_call_target="tpu_custom_call" | custom-call | tf_op jit(solution)/shard_map/lattice_steps/pallas_call | solution.py:551
  35.7 0.9 %write_out.1 = (f32[19,8,8,128]{3,2,1,0:T(8,128)}, f32[3,1088]{1,0:T(4,128)}) custom-call(f32[19,8,8,128]{3,2,1,0:T(8,128)S(1)} %get-tuple-element.4.pop_ref, f32[3,1088]{1,0:T(4,128)S(1)} %get-tuple-element.5.disp_ref), custom_call_target="tpu_custom_call" | custom-call | tf_op jit(solution)/shard_map/write_out/pallas_call | solution.py:609
